TPU v7x, 512 devices: a whole 4x8x8 slice. The times are simulated.
512 devices in a mesh: grp: 16 (over z, core), sub: 32 (over y, x).
Axes of the slice: x: 4, y: 8, z: 8, core: 2. Of those that a mesh axis runs over, the one named last changes fastest.
Arguments:
- right_side: float32 [8192, 512], P(('grp', 'sub')), may hold values from -8 to 8
- metric: float32 [8192, 1536], P(('grp', 'sub')), may hold values from 0.3 to 3
- helmholtz: float32 [8192, 512], P(('grp', 'sub')), may hold values from 0.5 to 2
- jacobi: float32 [8192, 512], P(('grp', 'sub')), may hold values from 0.05 to 0.5
- pair_list: int32 [2, 524288], P(None, ('grp', 'sub')), may hold values from 0 to 8191
- shared_slots: int32 [512, 32, 128], P(('grp', 'sub')), may hold values from 0 to 8192, as said below
- face_points: int32 [2, 262144], P(None, ('grp', 'sub')), may hold values from 0 to 8191
- coarse_map: int32 [8, 8192], P(None, ('grp', 'sub')), may hold values from 0 to 63
- coarse_inverse: float32 [16, 64, 64], P('grp'), as said below
Outputs:
- solution: float32 [8192, 512], P(('grp', 'sub'))
- residual: float32 [8192, 512], P(('grp', 'sub'))
Inputs may be any that keep to these rules, and one draw needn't show every extreme that they name: `shared_slots`: entries equal to 8192 mark empty slots; the slot of device a for peer b in one group is filled exactly when the slot of b for a at the same position is; a device's slots for itself are empty; filled slots come first in each row. `coarse_inverse`: each group's matrix is symmetric and positive definite.
All inputs are finite; a program needn't handle non-finite values.
Results may differ from a plain program's by a relative error of at most 0.0003.
Values sent between devices are 32-bit elements; how exact they have to be, the bound alone decides.
A program may use at most 64 MiB of HBM per device.

v0:
```python
import jax
import jax.numpy as jnp
import numpy as np
from jax import lax
from jax.sharding import PartitionSpec as P

ITERS = 2
NC = 64


def extended(cells, sides, width):
    for axis, dim in sides:
        count = lax.axis_size(axis)
        ends = count - 1
        head = lax.slice_in_dim(cells, 0, width, axis=dim)
        tail = lax.slice_in_dim(cells, cells.shape[dim] - width, cells.shape[dim], axis=dim)
        cells = jnp.concatenate(
            [
                lax.ppermute(tail, axis, [(i, (i + 1) % count) for i in range(ends)]),
                cells,
                lax.ppermute(head, axis, [((i + 1) % count, i) for i in range(ends)]),
            ],
            axis=dim,
        )
    return cells


def tables():
    order_index = np.arange(8)
    colloc = np.cos(np.pi * order_index / 7.0)
    end_weights = (
        np.where((order_index == 0) | (order_index == 7), 2.0, 1.0) * (-1.0) ** order_index
    )
    spacing = colloc[:, None] - colloc[None, :] + np.eye(8)
    raw_matrix = np.outer(end_weights, 1.0 / end_weights) / spacing
    off_part = raw_matrix * (1.0 - np.eye(8))
    derivative = 0.25 * (off_part - np.eye(8) * off_part.sum(axis=1)[:, None])
    along_first = np.kron(derivative, np.eye(64)).T
    along_inner = np.concatenate(
        [np.kron(derivative, np.eye(8)).T, np.kron(np.eye(8), derivative).T], axis=1
    )
    point_index = np.arange(512)
    corner_index = np.arange(8)
    sign_first = 1.0 - 2.0 * (corner_index >> 2 & 1)
    sign_second = 1.0 - 2.0 * (corner_index >> 1 & 1)
    sign_third = 1.0 - 2.0 * (corner_index & 1)
    node_first = colloc[point_index // 64][:, None]
    node_second = colloc[point_index // 8 % 8][:, None]
    node_third = colloc[point_index % 8][:, None]
    corner = (
        0.5
        * (1.0 + sign_first[None, :] * node_first)
        * (0.5 * (1.0 + sign_second[None, :] * node_second))
        * (0.5 * (1.0 + sign_third[None, :] * node_third))
    )
    return (
        jnp.asarray(along_first, jnp.float32),
        jnp.asarray(along_inner, jnp.float32),
        jnp.asarray(corner, jnp.float32),
    )


def residual_product(resid, smoothed):
    return lax.psum(jnp.sum(resid * smoothed), ("grp", "sub"))


def body(
    right_side,
    metric,
    helmholtz,
    jacobi,
    pair_list,
    shared_slots,
    face_points,
    coarse_map,
    coarse_inverse,
):
    highest = lax.Precision.HIGHEST
    along_first, along_inner, corner = tables()
    elements = right_side.shape[0]
    points = elements * right_side.shape[1]
    slots = shared_slots[0]

    def assemble(field):
        flat = field.reshape(-1)
        total = (
            flat.at[pair_list[0]].add(flat[pair_list[1]]).at[pair_list[1]].add(flat[pair_list[0]])
        )
        padded = jnp.concatenate([flat, jnp.zeros((1,), jnp.float32)])
        sent = padded[slots]
        received = lax.all_to_all(sent, "sub", split_axis=0, concat_axis=0, tiled=True)
        total = (
            jnp.concatenate([total, jnp.zeros((1,), jnp.float32)]).at[slots].add(received)[:points]
        )
        face_values = flat[face_points]
        rim = extended(face_values, (("grp", 0),), 1)
        total = total.at[face_points[0]].add(rim[0]).at[face_points[1]].add(rim[3])
        return total.reshape(field.shape)

    onehot = (coarse_map.reshape(-1)[:, None] == jnp.arange(NC, dtype=jnp.int32)[None, :]).astype(
        jnp.float32
    )

    def precondition(resid):
        vertex = jnp.dot(resid, corner, precision=highest)
        partial_coarse = jnp.dot(vertex.T.reshape(-1), onehot, precision=highest)
        coarse = lax.psum(partial_coarse, "sub")
        solved = jnp.dot(coarse_inverse[0], coarse, precision=highest)
        at_vertex = jnp.dot(onehot, solved, precision=highest).reshape(8, -1)
        return jacobi * resid + jnp.dot(at_vertex.T, corner.T, precision=highest)

    solution = jnp.zeros_like(right_side)
    residual = right_side
    smoothed = precondition(residual)
    direction = smoothed
    rz_now = residual_product(residual, smoothed)
    for iteration in range(ITERS):
        summed = assemble(direction)
        grad_first = jnp.dot(summed, along_first, precision=highest)
        inner = jnp.dot(summed.reshape(elements * 8, 64), along_inner, precision=highest)
        grad_second = inner[:, :64].reshape(elements, 512)
        grad_third = inner[:, 64:].reshape(elements, 512)
        flux_first = metric[:, :512] * grad_first
        flux_second = (metric[:, 512:1024] * grad_second).reshape(elements * 8, 64)
        flux_third = (metric[:, 1024:] * grad_third).reshape(elements * 8, 64)
        back = jnp.dot(flux_first, along_first.T, precision=highest)
        fluxes = jnp.concatenate([flux_second, flux_third], axis=1)
        back = back + jnp.dot(fluxes, along_inner.T, precision=highest).reshape(elements, 512)
        image = assemble(back) + helmholtz * direction
        alpha = rz_now / lax.psum(jnp.sum(direction * image), ("grp", "sub"))
        solution = solution + alpha * direction
        residual = residual - alpha * image
        if iteration + 1 < ITERS:
            smoothed = precondition(residual)
            rz_new = residual_product(residual, smoothed)
            direction = smoothed + rz_new / rz_now * direction
            rz_now = rz_new
    return (solution, residual)


def solution(mesh):
    in_specs = (
        P(("grp", "sub"), None),
        P(("grp", "sub"), None),
        P(("grp", "sub"), None),
        P(("grp", "sub"), None),
        P(None, ("grp", "sub")),
        P(("grp", "sub"), None, None),
        P(None, ("grp", "sub")),
        P(None, ("grp", "sub")),
        P("grp", None, None),
    )
    out_specs = (P(("grp", "sub"), None), P(("grp", "sub"), None))
    return jax.shard_map(body, mesh=mesh, in_specs=in_specs, out_specs=out_specs, check_vma=False)
```

profile of v0, /device:TPU:1, one launch (start us, length us, event | category | flops | bytes accessed | tf_op | source)
XLA Modules:
  0.0 937.5 jit_solution(3076881587278794797)
XLA Ops:
  3.3 61.9 %psum.42 = f32[64]{0:T(128)S(1)} all-reduce(f32[64]{0:T(128)S(1)} %convolution_bitcast_fusion.5), channel_id=1, replica_groups=mesh['grp'=16,'sub'=32] {'sub'}, use_global_device_ids=true, to_apply=%region_0.0 | all-reduce | flops 64 | bytes 512 | tf_op jit(solution)/shard_map/psum | solution.py:107
  67.3 40.6 %gather_fusion.2 = f32[4096]{0:T(1024)} fusion(f32[8193]{0:T(1024)S(1)} %pad_maximum_fusion.6, s32[4096]{0:T(1024)S(1)} %broadcast_clamp_fusion), kind=kCustom, calls=%fused_computation.2 | custom fusion | bytes 49152 | tf_op jit(solution)/shard_map/gather | solution.py:90
  107.8 4.3 all-to-all-start
  112.2 6.2 gather_fusion.3
  118.4 19.0 %collective-permute-start = (f32[1,512]{1,0:T(1,128)S(1)}, f32[1,512]{1,0:T(1,128)S(1)}, u32[]{:S(2)}, u32[]{:S(2)}) collective-permute-start(f32[1,512]{1,0:T(1,128)S(1)} %bitcast.169), channel_id=1, source_target_pairs={{0,32},{32,64},{64,96},{96,128},{128,160},{160,192},{192,224},{224... | collective-permute-start | bytes 6152 | tf_op jit(solution)/shard_map/ppermute | solution.py:19
  139.4 6.2 gather_fusion
  145.6 6.2 gather_fusion.1
  151.7 6.1 scatter_fusion
  157.9 6.1 scatter_fusion.1
  164.0 26.0 %scatter_fusion.2 = f32[8193]{0:T(1024)S(1)} fusion(f32[8193]{0:T(1024)S(1)} %pad_maximum_fusion.7, s32[4096]{0:T(1024)S(1)} %fusion.8, f32[4096]{0:T(1024)S(1)} %bitcast.146), kind=kCustom, calls=%fused_computation.18 | custom fusion | flops 4096 | bytes 65536 | tf_op jit(solution)/shard_map/scatter-add | solution.py:93
  193.5 3.8 scatter_fusion.4
  201.8 6.2 gather_fusion.4
  207.9 6.2 gather_fusion.5
  214.1 6.2 gather_fusion.7
  220.3 40.6 %gather_fusion.6 = f32[4096]{0:T(1024)} fusion(f32[8193]{0:T(1024)S(1)} %pad_maximum_fusion.4, s32[4096]{0:T(1024)S(1)} %broadcast_clamp_fusion), kind=kCustom, calls=%fused_computation.6 | custom fusion | bytes 49152 | tf_op jit(solution)/shard_map/gather | solution.py:90
  260.8 6.1 scatter_fusion.5
  266.9 6.1 scatter_fusion.6
  273.0 9.4 %all-to-all-start.1 = ((f32[32,1,128]{2,1,0:T(1,128)}), f32[32,1,128]{2,1,0:T(1,128)S(1)}, u32[]{:S(2)}, u32[]{:S(2)}) async-start(f32[32,1,128]{2,1,0:T(1,128)} %bitcast.22), calls=%async_computation.1 | async-start | bytes 32768 | tf_op jit(solution)/shard_map/all_to_all | solution.py:91
  282.4 3.9 collective-permute-start.2
  290.9 26.0 %scatter_fusion.7 = f32[8193]{0:T(1024)S(1)} fusion(f32[8193]{0:T(1024)S(1)} %pad_maximum_fusion.5, s32[4096]{0:T(1024)S(1)} %fusion.8, f32[4096]{0:T(1024)S(1)} %bitcast.148), kind=kCustom, calls=%fused_computation.23 | custom fusion | flops 4096 | bytes 65536 | tf_op jit(solution)/shard_map/scatter-add | solution.py:93
  317.0 3.4 scatter_fusion.8
  320.4 3.4 scatter_fusion.9
  325.1 101.2 %all-reduce = (f32[]{:T(128)}, f32[]{:T(128)}) all-reduce(f32[]{:T(128)} %get-tuple-element.3, f32[]{:T(128)} %get-tuple-element.2), channel_id=1, replica_groups=mesh['grp'=16,'sub'=32] {'grp','sub'}, use_global_device_ids=true, to_apply=%region_2.0 | all-reduce | flops 2 | bytes 16 | tf_op jit(solution)/shard_map/psum | solution.py:64
  428.5 56.9 %psum.45 = f32[64]{0:T(128)S(1)} all-reduce(f32[64]{0:T(128)S(1)} %convolution_bitcast_fusion.2), channel_id=1, replica_groups=mesh['grp'=16,'sub'=32] {'sub'}, use_global_device_ids=true, to_apply=%region_15.0 | all-reduce | flops 64 | bytes 512 | tf_op jit(solution)/shard_map/psum | solution.py:107
  486.9 107.3 %psum.46 = f32[]{:T(128)} all-reduce(f32[]{:T(128)} %get-tuple-element.28), channel_id=1, replica_groups=mesh['grp'=16,'sub'=32] {'grp','sub'}, use_global_device_ids=true, to_apply=%region_17.0 | all-reduce | flops 1 | bytes 8 | tf_op jit(solution)/shard_map/psum | solution.py:64
  595.7 6.2 gather_fusion.8
  601.8 6.2 gather_fusion.9
  608.0 6.2 gather_fusion.11
  614.2 40.6 %gather_fusion.10 = f32[4096]{0:T(1024)} fusion(f32[8193]{0:T(1024)S(1)} %pad_maximum_fusion.2, s32[4096]{0:T(1024)S(1)} %broadcast_clamp_fusion), kind=kCustom, calls=%fused_computation.10 | custom fusion | bytes 49152 | tf_op jit(solution)/shard_map/gather | solution.py:90
  654.7 6.1 scatter_fusion.10
  660.8 6.1 scatter_fusion.11
  666.9 7.2 all-to-all-start.2
  674.1 4.7 collective-permute-start.4
  682.7 26.0 %scatter_fusion.12 = f32[8193]{0:T(1024)S(1)} fusion(f32[8193]{0:T(1024)S(1)} %pad_maximum_fusion.3, s32[4096]{0:T(1024)S(1)} %fusion.8, f32[4096]{0:T(1024)S(1)} %bitcast.149), kind=kCustom, calls=%fused_computation.28 | custom fusion | flops 4096 | bytes 65536 | tf_op jit(solution)/shard_map/scatter-add | solution.py:93
  708.7 3.4 scatter_fusion.13
  712.1 3.6 scatter_fusion.14
  718.9 6.2 gather_fusion.12
  725.1 6.2 gather_fusion.13
  731.2 6.2 gather_fusion.15
  737.4 40.6 %gather_fusion.14 = f32[4096]{0:T(1024)} fusion(f32[8193]{0:T(1024)S(1)} %pad_maximum_fusion, s32[4096]{0:T(1024)S(1)} %broadcast_clamp_fusion), kind=kCustom, calls=%fused_computation.14 | custom fusion | bytes 49152 | tf_op jit(solution)/shard_map/gather | solution.py:90
  778.0 6.1 scatter_fusion.15
  784.1 6.1 scatter_fusion.16
  790.2 7.6 all-to-all-start.3
  797.8 3.9 collective-permute-start.6
  806.3 26.0 %scatter_fusion.17 = f32[8193]{0:T(1024)S(1)} fusion(f32[8193]{0:T(1024)S(1)} %pad_maximum_fusion.1, s32[4096]{0:T(1024)S(1)} %fusion.8, f32[4096]{0:T(1024)S(1)} %bitcast.147), kind=kCustom, calls=%fused_computation.33 | custom fusion | flops 4096 | bytes 65536 | tf_op jit(solution)/shard_map/scatter-add | solution.py:93
  832.3 3.4 scatter_fusion.18
  835.7 3.4 scatter_fusion.19
  839.7 95.6 %psum.47 = f32[]{:T(128)} all-reduce(f32[]{:T(128)} %multiply_reduce_fusion), channel_id=1, replica_groups=mesh['grp'=16,'sub'=32] {'grp','sub'}, use_global_device_ids=true, to_apply=%region_29.0 | all-reduce | flops 1 | bytes 8 | tf_op jit(solution)/shard_map/psum | solution.py:130
  (128 shorter events, 35.5 us)
Async XLA Ops:
  0.6 64.6 %copy-start = (f32[1,64,64]{2,1,0:T(8,128)S(1)}, f32[1,64,64]{2,1,0:T(8,128)}, u32[]{:S(2)}) copy-start(f32[1,64,64]{2,1,0:T(8,128)} %param.20) | copy-start | bytes 49156
  0.6 65.0 %copy-start.2 = (f32[512,8]{1,0:T(8,128)S(1)}, f32[512,8]{1,0:T(8,128)}, u32[]{:S(2)}) copy-start(f32[512,8]{1,0:T(8,128)} %constant.5.clone) | copy-start | bytes 49156
  65.3 0.8 copy-start.3
  65.3 0.8 copy-start.6
  66.5 0.7 copy-start.10
  107.8 4.3 copy-start.11
  107.8 56.2 %all-to-all-start = ((f32[32,1,128]{2,1,0:T(1,128)}), f32[32,1,128]{2,1,0:T(1,128)S(1)}, u32[]{:S(2)}, u32[]{:S(2)}) async-start(f32[32,1,128]{2,1,0:T(1,128)} %bitcast.12), calls=%async_computation | async-start | bytes 32768 | tf_op jit(solution)/shard_map/all_to_all | solution.py:91
  118.4 71.7 %collective-permute-start = (f32[1,512]{1,0:T(1,128)S(1)}, f32[1,512]{1,0:T(1,128)S(1)}, u32[]{:S(2)}, u32[]{:S(2)}) collective-permute-start(f32[1,512]{1,0:T(1,128)S(1)} %bitcast.169), channel_id=1, source_target_pairs={{0,32},{32,64},{64,96},{96,128},{128,160},{160,192},{192,224},{224... | collective-permute-start | bytes 6152 | tf_op jit(solution)/shard_map/ppermute | solution.py:19
  137.4 2.0 copy-start.12
  137.4 56.0 %collective-permute-start.1 = (f32[1,512]{1,0:T(1,128)S(1)}, f32[1,512]{1,0:T(1,128)S(1)}, u32[]{:S(2)}, u32[]{:S(2)}) collective-permute-start(f32[1,512]{1,0:T(1,128)S(1)} %bitcast.167), channel_id=1, source_target_pairs={{32,0},{64,32},{96,64},{128,96},{160,128},{192,160},{224,192},{256... | collective-permute-start | bytes 6152 | tf_op jit(solution)/shard_map/ppermute | solution.py:21
  193.4 4.0 copy-start.8
  193.5 4.6 copy-start.5
  197.3 2.8 copy-start.1
  198.2 0.8 copy-start.9
  199.0 0.8 copy-start.7
  273.0 17.9 %all-to-all-start.1 = ((f32[32,1,128]{2,1,0:T(1,128)}), f32[32,1,128]{2,1,0:T(1,128)S(1)}, u32[]{:S(2)}, u32[]{:S(2)}) async-start(f32[32,1,128]{2,1,0:T(1,128)} %bitcast.22), calls=%async_computation.1 | async-start | bytes 32768 | tf_op jit(solution)/shard_map/all_to_all | solution.py:91
  282.4 34.5 %collective-permute-start.2 = (f32[1,512]{1,0:T(1,128)S(1)}, f32[1,512]{1,0:T(1,128)S(1)}, u32[]{:S(2)}, u32[]{:S(2)}) collective-permute-start(f32[1,512]{1,0:T(1,128)S(1)} %bitcast.173), channel_id=1, source_target_pairs={{0,32},{32,64},{64,96},{96,128},{128,160},{160,192},{192,224},{224... | collective-permute-start | bytes 6152 | tf_op jit(solution)/shard_map/ppermute | solution.py:19
  286.3 34.0 %collective-permute-start.3 = (f32[1,512]{1,0:T(1,128)S(1)}, f32[1,512]{1,0:T(1,128)S(1)}, u32[]{:S(2)}, u32[]{:S(2)}) collective-permute-start(f32[1,512]{1,0:T(1,128)S(1)} %bitcast.170), channel_id=1, source_target_pairs={{32,0},{64,32},{96,64},{128,96},{160,128},{192,160},{224,192},{256... | collective-permute-start | bytes 6152 | tf_op jit(solution)/shard_map/ppermute | solution.py:21
  323.8 0.8 copy-start.4
  666.9 15.7 %all-to-all-start.2 = ((f32[32,1,128]{2,1,0:T(1,128)}), f32[32,1,128]{2,1,0:T(1,128)S(1)}, u32[]{:S(2)}, u32[]{:S(2)}) async-start(f32[32,1,128]{2,1,0:T(1,128)} %bitcast.33), calls=%async_computation.2 | async-start | bytes 32768 | tf_op jit(solution)/shard_map/all_to_all | solution.py:91
  674.1 34.5 %collective-permute-start.4 = (f32[1,512]{1,0:T(1,128)S(1)}, f32[1,512]{1,0:T(1,128)S(1)}, u32[]{:S(2)}, u32[]{:S(2)}) collective-permute-start(f32[1,512]{1,0:T(1,128)S(1)} %bitcast.174), channel_id=1, source_target_pairs={{0,32},{32,64},{64,96},{96,128},{128,160},{160,192},{192,224},{224... | collective-permute-start | bytes 6152 | tf_op jit(solution)/shard_map/ppermute | solution.py:19
  678.9 33.2 %collective-permute-start.5 = (f32[1,512]{1,0:T(1,128)S(1)}, f32[1,512]{1,0:T(1,128)S(1)}, u32[]{:S(2)}, u32[]{:S(2)}) collective-permute-start(f32[1,512]{1,0:T(1,128)S(1)} %bitcast.171), channel_id=1, source_target_pairs={{32,0},{64,32},{96,64},{128,96},{160,128},{192,160},{224,192},{256... | collective-permute-start | bytes 6152 | tf_op jit(solution)/shard_map/ppermute | solution.py:21
  790.2 16.1 %all-to-all-start.3 = ((f32[32,1,128]{2,1,0:T(1,128)}), f32[32,1,128]{2,1,0:T(1,128)S(1)}, u32[]{:S(2)}, u32[]{:S(2)}) async-start(f32[32,1,128]{2,1,0:T(1,128)} %bitcast.39), calls=%async_computation.3 | async-start | bytes 32768 | tf_op jit(solution)/shard_map/all_to_all | solution.py:91
  797.8 34.5 %collective-permute-start.6 = (f32[1,512]{1,0:T(1,128)S(1)}, f32[1,512]{1,0:T(1,128)S(1)}, u32[]{:S(2)}, u32[]{:S(2)}) collective-permute-start(f32[1,512]{1,0:T(1,128)S(1)} %bitcast.172), channel_id=1, source_target_pairs={{0,32},{32,64},{64,96},{96,128},{128,160},{160,192},{192,224},{224... | collective-permute-start | bytes 6152 | tf_op jit(solution)/shard_map/ppermute | solution.py:19
  801.6 34.1 %collective-permute-start.7 = (f32[1,512]{1,0:T(1,128)S(1)}, f32[1,512]{1,0:T(1,128)S(1)}, u32[]{:S(2)}, u32[]{:S(2)}) collective-permute-start(f32[1,512]{1,0:T(1,128)S(1)} %bitcast.168), channel_id=1, source_target_pairs={{32,0},{64,32},{96,64},{128,96},{160,128},{192,160},{224,192},{256... | collective-permute-start | bytes 6152 | tf_op jit(solution)/shard_map/ppermute | solution.py:21
where the time goes:
time: 945 us; the launch traced here: 938 us
  blocking collectives  423 us (45%)
  local copies, waits for them, and re-layouts  242 us (26%)
  other arithmetic  183 us (19%)
  starting transfers between devices  67.7 us (7%)
    psum x2, blocking collectives, residual_product(): return lax.psum(jnp.sum(resid * smoothed), ('grp', 'sub'))  209 us
    gather x4, local copies, waits for them, and re-layouts, assemble(): sent = padded[slots]  162 us
    psum x2, blocking collectives, precondition(): coarse = lax.psum(partial_coarse, 'sub')  119 us
    scatter-add x4, other arithmetic, assemble(): jnp.concatenate([total, jnp.zeros((1,), jnp.float32)]).at[slots]  104 us
    psum x1, blocking collectives, body(): alpha = rz_now / lax.psum(jnp.sum(direction * image), ('grp', 'sub'))  95.6 us
    scatter-add x8, other arithmetic, assemble(): flat.at[pair_list[0]].add(flat[pair_list[1]]).at[pair_list[1]]  48.8 us
    ppermute x4, starting transfers between devices, extended(): lax.ppermute(tail, axis, [(i, (i + 1) % count) for i in range(ends)])  31.5 us
    all_to_all x4, starting transfers between devices, assemble(): lax.all_to_all(sent, 'sub', split_axis=0, concat_axis=0, tiled=True)  28.5 us
  transfers between devices with their start and end apart: 12, of which 3 were waited for; matrix products, arithmetic and copies ran while one was open for 16% of the time, Pallas kernels for 0%

commit v1 on v0

--- a/solution.py
+++ b/solution.py
@@ -104,7 +104,9 @@
     def precondition(resid):
         vertex = jnp.dot(resid, corner, precision=highest)
         partial_coarse = jnp.dot(vertex.T.reshape(-1), onehot, precision=highest)
-        coarse = lax.psum(partial_coarse, "sub")
+        coarse = partial_coarse
+        for hop in (1, 2, 4, 8, 16):
+            coarse = coarse + lax.ppermute(coarse, "sub", [(dev, dev ^ hop) for dev in range(32)])
         solved = jnp.dot(coarse_inverse[0], coarse, precision=highest)
         at_vertex = jnp.dot(onehot, solved, precision=highest).reshape(8, -1)
         return jacobi * resid + jnp.dot(at_vertex.T, corner.T, precision=highest)

time: 945 us -> 871 us (0.922)
  blocking collectives: 423 us -> 297 us
  starting transfers between devices: 67.7 us -> 100 us
  waiting for transfers between devices: 7.23 us -> 25.4 us
    psum x2 -> x0, blocking collectives: 119 us -> none  [precondition(): coarse = lax.psum(partial_coarse, 'sub')]
    ppermute x0 -> x10, starting transfers between devices: none -> 38.7 us  [precondition(): lax.ppermute(coarse, 'sub', [(dev, dev ^ hop) for dev in range(32)])]
    ppermute x0 -> x10, waiting for transfers between devices: none -> 16.5 us  [precondition(): lax.ppermute(coarse, 'sub', [(dev, dev ^ hop) for dev in range(32)])]
    ppermute x4, starting transfers between devices: 31.5 us -> 21.5 us  [extended(): lax.ppermute(tail, axis, [(i, (i + 1) % count) for i in range(ends)])]
  transfers between devices with their start and end apart: 12 -> 22, of which waited for: 3 -> 12; matrix products, arithmetic and copies ran while one was open for 16% -> 14% of each run, Pallas kernels for 0% -> 0%
where the time goes in v1:
time: 871 us; the launch traced here: 863 us
  blocking collectives  297 us (34%)
  local copies, waits for them, and re-layouts  243 us (28%)
  other arithmetic  183 us (21%)
  starting transfers between devices  100 us (11%)
  waiting for transfers between devices  25.4 us (3%)
  matrix products  9.39 us (1%)
    psum x2, blocking collectives, residual_product(): return lax.psum(jnp.sum(resid * smoothed), ('grp', 'sub'))  200 us
    gather x4, local copies, waits for them, and re-layouts, assemble(): sent = padded[slots]  162 us
    scatter-add x4, other arithmetic, assemble(): jnp.concatenate([total, jnp.zeros((1,), jnp.float32)]).at[slots]  104 us
    psum x1, blocking collectives, body(): alpha = rz_now / lax.psum(jnp.sum(direction * image), ('grp', 'sub'))  97 us
    scatter-add x8, other arithmetic, assemble(): flat.at[pair_list[0]].add(flat[pair_list[1]]).at[pair_list[1]]  48.8 us
    ppermute x10, starting transfers between devices, precondition(): lax.ppermute(coarse, 'sub', [(dev, dev ^ hop) for dev in range(32)])  38.7 us
    all_to_all x4, starting transfers between devices, assemble(): lax.all_to_all(sent, 'sub', split_axis=0, concat_axis=0, tiled=True)  32.3 us
    scatter-add x8, other arithmetic, assemble(): total = total.at[face_points[0]].add(rim[0]).at[face_points[1]].add(rim[3])  27.7 us
  transfers between devices with their start and end apart: 22, of which 12 were waited for; matrix products, arithmetic and copies ran while one was open for 14% of the time, Pallas kernels for 0%

profile of v1, /device:TPU:1, one launch (start us, length us, event | category | flops | bytes accessed | tf_op | source)
XLA Modules:
  0.0 863.1 jit_solution(16011451052271724641)
XLA Ops:
  3.3 4.0 collective-permute-start
  8.7 4.4 collective-permute-start.1
  18.8 4.2 collective-permute-start.3
  23.9 7.4 collective-permute-start.4
  33.6 6.2 gather_fusion
  39.8 6.2 gather_fusion.1
  46.0 6.2 gather_fusion.3
  52.1 6.1 scatter_fusion
  58.3 6.1 scatter_fusion.1
  64.4 40.6 %gather_fusion.2 = f32[4096]{0:T(1024)} fusion(f32[8193]{0:T(1024)S(1)} %pad_maximum_fusion.6, s32[4096]{0:T(1024)S(1)} %broadcast_clamp_fusion), kind=kCustom, calls=%fused_computation.2 | custom fusion | bytes 49152 | tf_op jit(solution)/shard_map/gather | solution.py:90
  104.9 9.2 %all-to-all-start = ((f32[32,1,128]{2,1,0:T(1,128)}), f32[32,1,128]{2,1,0:T(1,128)S(1)}, u32[]{:S(2)}, u32[]{:S(2)}) async-start(f32[32,1,128]{2,1,0:T(1,128)} %bitcast.12), calls=%async_computation | async-start | bytes 32768 | tf_op jit(solution)/shard_map/all_to_all | solution.py:91
  114.2 10.6 %collective-permute-start.5 = (f32[1,512]{1,0:T(1,128)S(1)}, f32[1,512]{1,0:T(1,128)S(1)}, u32[]{:S(2)}, u32[]{:S(2)}) collective-permute-start(f32[1,512]{1,0:T(1,128)S(1)} %bitcast.172), channel_id=1, source_target_pairs={{0,32},{32,64},{64,96},{96,128},{128,160},{160,192},{192,224},{224... | collective-permute-start | bytes 6152 | tf_op jit(solution)/shard_map/ppermute | solution.py:19
  126.7 26.0 %scatter_fusion.2 = f32[8193]{0:T(1024)S(1)} fusion(f32[8193]{0:T(1024)S(1)} %pad_maximum_fusion.7, s32[4096]{0:T(1024)S(1)} %fusion.8, f32[4096]{0:T(1024)S(1)} %bitcast.147), kind=kCustom, calls=%fused_computation.18 | custom fusion | flops 4096 | bytes 65536 | tf_op jit(solution)/shard_map/scatter-add | solution.py:93
  156.2 3.8 scatter_fusion.4
  164.5 6.2 gather_fusion.4
  170.6 6.2 gather_fusion.5
  176.8 6.2 gather_fusion.7
  183.0 40.6 %gather_fusion.6 = f32[4096]{0:T(1024)} fusion(f32[8193]{0:T(1024)S(1)} %pad_maximum_fusion.4, s32[4096]{0:T(1024)S(1)} %broadcast_clamp_fusion), kind=kCustom, calls=%fused_computation.6 | custom fusion | bytes 49152 | tf_op jit(solution)/shard_map/gather | solution.py:90
  223.5 6.1 scatter_fusion.5
  229.6 6.1 scatter_fusion.6
  235.7 9.4 %all-to-all-start.1 = ((f32[32,1,128]{2,1,0:T(1,128)}), f32[32,1,128]{2,1,0:T(1,128)S(1)}, u32[]{:S(2)}, u32[]{:S(2)}) async-start(f32[32,1,128]{2,1,0:T(1,128)} %bitcast.22), calls=%async_computation.1 | async-start | bytes 32768 | tf_op jit(solution)/shard_map/all_to_all | solution.py:91
  245.1 3.9 collective-permute-start.7
  253.6 26.0 %scatter_fusion.7 = f32[8193]{0:T(1024)S(1)} fusion(f32[8193]{0:T(1024)S(1)} %pad_maximum_fusion.5, s32[4096]{0:T(1024)S(1)} %fusion.8, f32[4096]{0:T(1024)S(1)} %bitcast.148), kind=kCustom, calls=%fused_computation.23 | custom fusion | flops 4096 | bytes 65536 | tf_op jit(solution)/shard_map/scatter-add | solution.py:93
  279.7 3.4 scatter_fusion.8
  287.8 101.2 %all-reduce = (f32[]{:T(128)}, f32[]{:T(128)}) all-reduce(f32[]{:T(128)} %get-tuple-element.3, f32[]{:T(128)} %get-tuple-element.2), channel_id=1, replica_groups=mesh['grp'=16,'sub'=32] {'grp','sub'}, use_global_device_ids=true, to_apply=%region_1.0 | all-reduce | flops 2 | bytes 16 | tf_op jit(solution)/shard_map/psum | solution.py:64
  410.8 5.5 collective-permute-start.13
  420.5 98.9 %psum.30 = f32[]{:T(128)} all-reduce(f32[]{:T(128)} %get-tuple-element.28), channel_id=1, replica_groups=mesh['grp'=16,'sub'=32] {'grp','sub'}, use_global_device_ids=true, to_apply=%region_15.0 | all-reduce | flops 1 | bytes 8 | tf_op jit(solution)/shard_map/psum | solution.py:64
  520.8 6.2 gather_fusion.8
  526.9 6.2 gather_fusion.9
  533.1 6.2 gather_fusion.11
  539.2 40.6 %gather_fusion.10 = f32[4096]{0:T(1024)} fusion(f32[8193]{0:T(1024)S(1)} %pad_maximum_fusion.2, s32[4096]{0:T(1024)S(1)} %broadcast_clamp_fusion), kind=kCustom, calls=%fused_computation.10 | custom fusion | bytes 49152 | tf_op jit(solution)/shard_map/gather | solution.py:90
  579.8 6.1 scatter_fusion.10
  585.9 6.1 scatter_fusion.11
  592.0 7.7 all-to-all-start.2
  604.8 3.4 all-to-all-done.2
  608.2 26.0 %scatter_fusion.12 = f32[8193]{0:T(1024)S(1)} fusion(f32[8193]{0:T(1024)S(1)} %pad_maximum_fusion.3, s32[4096]{0:T(1024)S(1)} %fusion.8, f32[4096]{0:T(1024)S(1)} %bitcast.149), kind=kCustom, calls=%fused_computation.28 | custom fusion | flops 4096 | bytes 65536 | tf_op jit(solution)/shard_map/scatter-add | solution.py:93
  634.3 3.4 scatter_fusion.13
  637.7 3.6 scatter_fusion.14
  644.5 6.2 gather_fusion.12
  650.7 6.2 gather_fusion.13
  656.8 6.2 gather_fusion.15
  663.0 40.6 %gather_fusion.14 = f32[4096]{0:T(1024)} fusion(f32[8193]{0:T(1024)S(1)} %pad_maximum_fusion, s32[4096]{0:T(1024)S(1)} %broadcast_clamp_fusion), kind=kCustom, calls=%fused_computation.14 | custom fusion | bytes 49152 | tf_op jit(solution)/shard_map/gather | solution.py:90
  703.6 6.1 scatter_fusion.15
  709.7 6.1 scatter_fusion.16
  715.8 6.0 all-to-all-start.3
  721.8 3.9 collective-permute-start.16
  730.3 26.0 %scatter_fusion.17 = f32[8193]{0:T(1024)S(1)} fusion(f32[8193]{0:T(1024)S(1)} %pad_maximum_fusion.1, s32[4096]{0:T(1024)S(1)} %fusion.8, f32[4096]{0:T(1024)S(1)} %bitcast.146), kind=kCustom, calls=%fused_computation.33 | custom fusion | flops 4096 | bytes 65536 | tf_op jit(solution)/shard_map/scatter-add | solution.py:93
  763.8 97.0 %psum.31 = f32[]{:T(128)} all-reduce(f32[]{:T(128)} %multiply_reduce_fusion), channel_id=1, replica_groups=mesh['grp'=16,'sub'=32] {'grp','sub'}, use_global_device_ids=true, to_apply=%region_27.0 | all-reduce | flops 1 | bytes 8 | tf_op jit(solution)/shard_map/psum | solution.py:132
  (154 shorter events, 77.4 us)
Async XLA Ops:
  0.6 31.7 %copy-start = (f32[1,64,64]{2,1,0:T(8,128)S(1)}, f32[1,64,64]{2,1,0:T(8,128)}, u32[]{:S(2)}) copy-start(f32[1,64,64]{2,1,0:T(8,128)} %param.20) | copy-start | bytes 49156
  1.4 31.3 %copy-start.2 = (f32[512,8]{1,0:T(8,128)S(1)}, f32[512,8]{1,0:T(8,128)}, u32[]{:S(2)}) copy-start(f32[512,8]{1,0:T(8,128)} %constant.5.clone) | copy-start | bytes 49156
  3.1 4.2 copy-start.10
  3.3 5.4 collective-permute-start
  7.3 0.7 copy-start.12
  8.0 0.7 copy-start.11
  8.7 5.8 collective-permute-start.1
  14.5 4.3 collective-permute-start.2
  18.8 5.2 collective-permute-start.3
  23.9 8.4 collective-permute-start.4
  32.4 0.8 copy-start.3
  32.4 0.8 copy-start.6
  104.9 21.8 %all-to-all-start = ((f32[32,1,128]{2,1,0:T(1,128)}), f32[32,1,128]{2,1,0:T(1,128)S(1)}, u32[]{:S(2)}, u32[]{:S(2)}) async-start(f32[32,1,128]{2,1,0:T(1,128)} %bitcast.12), calls=%async_computation | async-start | bytes 32768 | tf_op jit(solution)/shard_map/all_to_all | solution.py:91
  114.2 38.6 %collective-permute-start.5 = (f32[1,512]{1,0:T(1,128)S(1)}, f32[1,512]{1,0:T(1,128)S(1)}, u32[]{:S(2)}, u32[]{:S(2)}) collective-permute-start(f32[1,512]{1,0:T(1,128)S(1)} %bitcast.172), channel_id=1, source_target_pairs={{0,32},{32,64},{64,96},{96,128},{128,160},{160,192},{192,224},{224... | collective-permute-start | bytes 6152 | tf_op jit(solution)/shard_map/ppermute | solution.py:19
  124.8 31.4 %collective-permute-start.6 = (f32[1,512]{1,0:T(1,128)S(1)}, f32[1,512]{1,0:T(1,128)S(1)}, u32[]{:S(2)}, u32[]{:S(2)}) collective-permute-start(f32[1,512]{1,0:T(1,128)S(1)} %bitcast.168), channel_id=1, source_target_pairs={{32,0},{64,32},{96,64},{128,96},{160,128},{192,160},{224,192},{256... | collective-permute-start | bytes 6152 | tf_op jit(solution)/shard_map/ppermute | solution.py:21
  156.1 4.0 copy-start.8
  156.2 4.6 copy-start.5
  160.0 2.8 copy-start.1
  160.9 0.8 copy-start.9
  161.7 0.8 copy-start.7
  235.7 17.9 %all-to-all-start.1 = ((f32[32,1,128]{2,1,0:T(1,128)}), f32[32,1,128]{2,1,0:T(1,128)S(1)}, u32[]{:S(2)}, u32[]{:S(2)}) async-start(f32[32,1,128]{2,1,0:T(1,128)} %bitcast.22), calls=%async_computation.1 | async-start | bytes 32768 | tf_op jit(solution)/shard_map/all_to_all | solution.py:91
  245.1 34.5 %collective-permute-start.7 = (f32[1,512]{1,0:T(1,128)S(1)}, f32[1,512]{1,0:T(1,128)S(1)}, u32[]{:S(2)}, u32[]{:S(2)}) collective-permute-start(f32[1,512]{1,0:T(1,128)S(1)} %bitcast.173), channel_id=1, source_target_pairs={{0,32},{32,64},{64,96},{96,128},{128,160},{160,192},{192,224},{224... | collective-permute-start | bytes 6152 | tf_op jit(solution)/shard_map/ppermute | solution.py:19
  249.0 34.0 %collective-permute-start.8 = (f32[1,512]{1,0:T(1,128)S(1)}, f32[1,512]{1,0:T(1,128)S(1)}, u32[]{:S(2)}, u32[]{:S(2)}) collective-permute-start(f32[1,512]{1,0:T(1,128)S(1)} %bitcast.169), channel_id=1, source_target_pairs={{32,0},{64,32},{96,64},{128,96},{160,128},{192,160},{224,192},{256... | collective-permute-start | bytes 6152 | tf_op jit(solution)/shard_map/ppermute | solution.py:21
  286.5 0.8 copy-start.4
  391.3 4.3 collective-permute-start.9
  395.6 5.8 collective-permute-start.10
  401.3 4.3 collective-permute-start.11
  405.6 5.2 collective-permute-start.12
  410.8 8.2 collective-permute-start.13
  592.0 16.2 %all-to-all-start.2 = ((f32[32,1,128]{2,1,0:T(1,128)}), f32[32,1,128]{2,1,0:T(1,128)S(1)}, u32[]{:S(2)}, u32[]{:S(2)}) async-start(f32[32,1,128]{2,1,0:T(1,128)} %bitcast.33), calls=%async_computation.2 | async-start | bytes 32768 | tf_op jit(solution)/shard_map/all_to_all | solution.py:91
  599.7 34.5 %collective-permute-start.14 = (f32[1,512]{1,0:T(1,128)S(1)}, f32[1,512]{1,0:T(1,128)S(1)}, u32[]{:S(2)}, u32[]{:S(2)}) collective-permute-start(f32[1,512]{1,0:T(1,128)S(1)} %bitcast.174), channel_id=1, source_target_pairs={{0,32},{32,64},{64,96},{96,128},{128,160},{160,192},{192,224},{224... | collective-permute-start | bytes 6152 | tf_op jit(solution)/shard_map/ppermute | solution.py:19
  602.9 34.8 %collective-permute-start.15 = (f32[1,512]{1,0:T(1,128)S(1)}, f32[1,512]{1,0:T(1,128)S(1)}, u32[]{:S(2)}, u32[]{:S(2)}) collective-permute-start(f32[1,512]{1,0:T(1,128)S(1)} %bitcast.170), channel_id=1, source_target_pairs={{32,0},{64,32},{96,64},{128,96},{160,128},{192,160},{224,192},{256... | collective-permute-start | bytes 6152 | tf_op jit(solution)/shard_map/ppermute | solution.py:21
  715.8 14.6 %all-to-all-start.3 = ((f32[32,1,128]{2,1,0:T(1,128)}), f32[32,1,128]{2,1,0:T(1,128)S(1)}, u32[]{:S(2)}, u32[]{:S(2)}) async-start(f32[32,1,128]{2,1,0:T(1,128)} %bitcast.39), calls=%async_computation.3 | async-start | bytes 32768 | tf_op jit(solution)/shard_map/all_to_all | solution.py:91
  721.8 34.6 %collective-permute-start.16 = (f32[1,512]{1,0:T(1,128)S(1)}, f32[1,512]{1,0:T(1,128)S(1)}, u32[]{:S(2)}, u32[]{:S(2)}) collective-permute-start(f32[1,512]{1,0:T(1,128)S(1)} %bitcast.171), channel_id=1, source_target_pairs={{0,32},{32,64},{64,96},{96,128},{128,160},{160,192},{192,224},{224... | collective-permute-start | bytes 6152 | tf_op jit(solution)/shard_map/ppermute | solution.py:19
  725.6 34.1 %collective-permute-start.17 = (f32[1,512]{1,0:T(1,128)S(1)}, f32[1,512]{1,0:T(1,128)S(1)}, u32[]{:S(2)}, u32[]{:S(2)}) collective-permute-start(f32[1,512]{1,0:T(1,128)S(1)} %bitcast.167), channel_id=1, source_target_pairs={{32,0},{64,32},{96,64},{128,96},{160,128},{192,160},{224,192},{256... | collective-permute-start | bytes 6152 | tf_op jit(solution)/shard_map/ppermute | solution.py:21
